TPU v7x, 128 devices: a whole 4x4x4 slice. The times are simulated.
128 devices in a mesh: row: 8 (over z, x_lo), col: 16 (over x_hi, y, core).
Axes of the slice: x: 4 (x_hi: 2, x_lo: 2; x = x_hi * 2 + x_lo), y: 4, z: 4, core: 2. Of those that a mesh axis runs over, the one named last changes fastest.
Arguments:
- t2_pairs: bfloat16 [8, 8, 16, 16, 64, 64], P('row', None, None, None, 'col'), may hold values from -6 to 6
- cycle_ints: bfloat16 [8192, 8192], P('row', 'col'), may hold values from -0.1875 to 0.1875
- eps_occ: float32 [8, 16], replicated, may hold values from -2 to -0.4
- eps_virt: float32 [8, 64], replicated, may hold values from 0.2 to 3
- occ_count: int32 [8], replicated, may hold values from 8 to 16, as said below
- virt_count: int32 [8], replicated, may hold values from 32 to 64, as said below
- window_irrep: int32 [1], replicated, may hold values from 0 to 7
Outputs:
- update: float32 [8192, 8192], P('row', 'col')
Inputs may be any that keep to these rules, and one draw needn't show every extreme that they name: `occ_count`: at least half of the slots; one irrep fills all 16, and another holds exactly the least. `virt_count`: at least half of the slots; one irrep fills all 64, and another holds exactly the least.
All inputs are finite; a program needn't handle non-finite values.
Results may differ from a plain program's by a relative error of at most 0.0003.
Values may be sent and summed in bfloat16 or wider, within the bound.
A program may use at most 128 MiB of HBM per device.

v0:
```python
import jax
import jax.numpy as jnp
from jax import lax
from jax.sharding import PartitionSpec as P

NIRREP = 8
OCC_CAP = 16
VIR_CAP = 64


def ph_vectors(eps_occ, eps_virt, occ_count, virt_count, window_irrep):
    irreps = jnp.arange(NIRREP, dtype=jnp.int32)
    partner = jnp.bitwise_xor(irreps, window_irrep[0])
    onehot = partner[:, None] == irreps[None, :]
    virt_rows = jnp.dot(onehot.astype(jnp.float32), eps_virt, precision=lax.Precision.HIGHEST)
    virt_live = jnp.sum(jnp.where(onehot, virt_count[None, :], 0), axis=1)
    energy = eps_occ[:, None, :] - virt_rows[:, :, None]
    slots_occ = jnp.arange(OCC_CAP, dtype=jnp.int32)
    slots_virt = jnp.arange(VIR_CAP, dtype=jnp.int32)
    live = (slots_occ[None, None, :] < occ_count[:, None, None]) & (
        slots_virt[None, :, None] < virt_live[:, None, None]
    )
    return (energy, live)


def per_device(t2_pairs, cycle_ints, eps_occ, eps_virt, occ_count, virt_count, window_irrep):
    irrep_local = t2_pairs.shape[0]
    virt_local = t2_pairs.shape[4]
    total = NIRREP * VIR_CAP * OCC_CAP
    energy, live = ph_vectors(eps_occ, eps_virt, occ_count, virt_count, window_irrep)
    row_index = lax.axis_index("row")
    col_index = lax.axis_index("col")
    first_irrep = row_index * irrep_local
    first_virt = col_index * virt_local
    zero_index = jnp.int32(0)
    source_live = lax.dynamic_slice(
        live, (first_irrep, first_virt, zero_index), (irrep_local, virt_local, OCC_CAP)
    )
    full_live = live.reshape(-1)
    ordered = jnp.transpose(t2_pairs, (0, 4, 2, 1, 5, 3)).reshape(
        irrep_local, virt_local, OCC_CAP, total
    )
    keep = source_live[:, :, :, None] & full_live[None, None, None, :]
    ordered = jnp.where(keep, ordered, jnp.zeros_like(ordered))
    moved = lax.all_to_all(ordered, "col", split_axis=3, concat_axis=1, tiled=True)
    amp_local = moved.reshape(irrep_local * VIR_CAP * OCC_CAP, moved.shape[3])
    amp_panel = lax.all_gather(amp_local, "row", axis=0, tiled=True)
    ints_panel = lax.all_gather(cycle_ints, "col", axis=1, tiled=True)
    cycle = jnp.dot(ints_panel, amp_panel, preferred_element_type=jnp.float32)
    rows_here = cycle.shape[0]
    cols_here = cycle.shape[1]
    flat_energy = energy.reshape(-1)
    row_start = row_index * rows_here
    col_start = col_index * cols_here
    row_energy = lax.dynamic_slice_in_dim(flat_energy, row_start, rows_here, 0)
    col_energy = lax.dynamic_slice_in_dim(flat_energy, col_start, cols_here, 0)
    row_live = lax.dynamic_slice_in_dim(full_live, row_start, rows_here, 0)
    col_live = lax.dynamic_slice_in_dim(full_live, col_start, cols_here, 0)
    denom = row_energy[:, None] + col_energy[None, :]
    return jnp.where(row_live[:, None] & col_live[None, :], cycle / denom, jnp.float32(0.0))


def solution(mesh):
    placed = (P("row", None, None, None, "col", None), P("row", "col"), P(), P(), P(), P(), P())
    return jax.shard_map(
        per_device, mesh=mesh, in_specs=placed, out_specs=P("row", "col"), check_vma=False
    )
```

profile of v0, /device:TPU:1, one launch (start us, length us, event | category | flops | bytes accessed | tf_op | source)
XLA Modules:
  0.0 408.3 jit_solution(13650713026373814684)
XLA Ops:
  6.5 0.0 copy-start
  6.5 0.0 all-gather.3.cloned.1.call-start
  7.2 0.8 select_reduce_fusion
  8.1 0.1 iota_compare_fusion.2
  8.1 0.7 iota_compare_fusion.3
  8.9 0.1 broadcast_and_fusion
  9.0 0.1 and.62
  9.2 7.9 %copy.20 = bf16[1,4,16,8,64,16]{5,4,3,2,1,0:T(8,128)(2,1)} copy(bf16[1,4,16,8,64,16]{4,1,5,2,3,0:T(4,128)(2,1)} %bitcast.23) | data formatting | bytes 2097152 | tf_op jit(solution)/shard_map/transpose | solution.py:40
  17.0 15.1 %reshape.106 = bf16[1,4,16,8192]{3,2,1,0:T(8,128)(2,1)S(1)} reshape(bf16[1,4,16,8,64,16]{5,4,3,2,1,0:T(8,128)(2,1)} %copy.20) | data formatting | bytes 2097152 | tf_op jit(solution)/shard_map/reshape | solution.py:40
  32.2 0.4 and_select_fusion
  32.6 8.3 %copy.21 = bf16[1,4,16,8192]{2,1,0,3:T(4,128)(2,1)} copy(bf16[1,4,16,8192]{3,2,1,0:T(8,128)(2,1)S(1)} %and_select_fusion) | data formatting | bytes 2097152 | tf_op jit(solution)/shard_map/jit(_where)/select_n | solution.py:44
  40.9 10.4 %reshape.108 = bf16[16,2,16384]{2,1,0:T(2,128)(2,1)S(1)} reshape(bf16[8192,1,4,16]{3,2,1,0:T(4,128)(2,1)} %bitcast.19) | data formatting | bytes 2097152
  51.3 25.2 %all_to_all.15 = bf16[16,2,16384]{2,1,0:T(2,128)(2,1)S(1)} all-to-all(bf16[16,2,16384]{2,1,0:T(2,128)(2,1)S(1)} %reshape.108), channel_id=1, replica_groups=mesh['row'=8,'col'=16] {'col'}, dimensions={0} | all-to-all | bytes 2097152 | tf_op jit(solution)/shard_map/all_to_all | solution.py:45
  76.5 7.5 %reshape.109 = bf16[8192,1,4,16]{3,2,1,0:T(4,128)(2,1)} reshape(bf16[16,2,16384]{2,1,0:T(2,128)(2,1)S(1)} %all_to_all.15) | data formatting | bytes 2097152
  84.0 0.0 copy-start.1
  84.0 8.6 %copy.25 = bf16[1,4,16,16,512]{4,3,2,1,0:T(8,128)(2,1)S(1)} copy(bf16[1,4,16,16,512]{2,1,4,3,0:T(4,128)(2,1)} %bitcast.20) | data formatting | bytes 2097152 | tf_op jit(solution)/shard_map/all_to_all | solution.py:45
  92.6 1.5 copy.23
  94.2 0.0 all-gather.3.cloned.1.call-update
  94.2 0.0 all-gather.5.cloned.1.call-start
  94.3 0.7 all-gather.5.cloned.1.call-update
  95.0 0.1 dynamic_slice.16
  95.0 0.0 copy-done
  95.0 0.2 fusion.1
  95.2 0.0 copy-done.1
  95.2 0.1 broadcast_subtract_fusion
  95.4 0.1 sub.20
  95.5 0.1 dynamic_slice.19
  95.6 165.7 %all-gather.3.cloned.1.call-done = bf16[8192,512]{1,0:T(8,128)(2,1)} async-done(((bf16[1024,512]{1,0:T(8,128)(2,1)}), bf16[8192,512]{1,0:T(8,128)(2,1)}) %all-gather.3.cloned.1.call-update) | async-done | bytes 8388624 | tf_op jit(solution)/shard_map/all_gather | solution.py:47
  261.3 122.6 %all-gather.5.cloned.1.call-done = bf16[1024,8192]{1,0:T(8,128)(2,1)} async-done(((bf16[1024,512]{1,0:T(8,128)(2,1)}), bf16[1024,8192]{1,0:T(8,128)(2,1)}) %all-gather.5.cloned.1.call-update) | async-done | bytes 16777232 | tf_op jit(solution)/shard_map/all_gather | solution.py:48
  383.9 15.7 %fusion = f32[1024,512]{0,1:T(8,128)S(1)} fusion(bf16[8192,512]{1,0:T(8,128)(2,1)} %all-gather.3.cloned.1.call-done, bf16[1024,8192]{1,0:T(8,128)(2,1)} %all-gather.5.cloned.1.call-done, f32[512]{0:T(512)S(1)} %dynamic_slice.19, f32[1024]{0:T(1024)S(1)} %dynamic_slice.18, pred[1024]{0:T(1024)(128)(4,1)S(1)} %dynamic_slice.15, ...), kind=kOutput, calls=%fused_computation.1 | convolution fusion | flops 8592031744 | bytes 27270656 | tf_op jit(solution)/shard_map/dot_general | solution.py:49
  399.6 1.8 copy.24
  (4 shorter events, 0.0 us)
Async XLA Ops:
  6.5 88.5 %copy-start = (f32[8,64]{1,0:T(8,128)S(1)}, f32[8,64]{1,0:T(8,128)}, u32[]{:S(2)}) copy-start(f32[8,64]{1,0:T(8,128)} %param.10) | copy-start | bytes 6148
  6.5 254.8 %all-gather.3.cloned.1.call-start = ((), (), s32[]{:S(2)}) async-start(), calls=%async_computation.1 | async-start | bytes 9437184 | tf_op jit(solution)/shard_map/all_gather | solution.py:47
  84.0 11.2 %copy-start.1 = (f32[8,16]{1,0:T(8,128)S(1)}, f32[8,16]{1,0:T(8,128)}, u32[]{:S(2)}) copy-start(f32[8,16]{1,0:T(8,128)} %param.9) | copy-start | bytes 1540
  94.2 289.7 %all-gather.5.cloned.1.call-start = ((), (), s32[]{:S(2)}) async-start(), calls=%async_computation.2 | async-start | bytes 17825792 | tf_op jit(solution)/shard_map/all_gather | solution.py:48
Sparse Core Ops, SparseCore 0:
  94.3 166.9 all-gather.2
  263.6 120.3 all-gather.4
where the time goes:
time: 409 us; the launch traced here: 408 us
  waiting for transfers between devices  289 us (71%)
  local copies, waits for them, and re-layouts  61.7 us (15%)
  blocking collectives  25.2 us (6%)
  matrix products  15.9 us (4%)
  between operations  14.2 us (3%)
    all_gather x1, waiting for transfers between devices, per_device(): amp_panel = lax.all_gather(amp_local, 'row', axis=0, tiled=True)  166 us
    all_gather x1, waiting for transfers between devices, per_device(): ints_panel = lax.all_gather(cycle_ints, 'col', axis=1, tiled=True)  123 us
    all_to_all x1, blocking collectives, per_device(): lax.all_to_all(ordered, 'col', split_axis=3, concat_axis=1, tiled=True)  25.2 us
    unnamed x6, local copies, waits for them, and re-layouts  18 us
    dot_general x1, matrix products, per_device(): cycle = jnp.dot(ints_panel, amp_panel, preferred_element_type=jnp.float32)  15.7 us
    reshape x1, local copies, waits for them, and re-layouts, per_device(): jnp.transpose(t2_pairs, (0, 4, 2, 1, 5, 3))  15.1 us
    all_to_all x2, local copies, waits for them, and re-layouts, per_device(): lax.all_to_all(ordered, 'col', split_axis=3, concat_axis=1, tiled=True)  10.1 us
    select_n x1, local copies, waits for them, and re-layouts, per_device(): ordered = jnp.where(keep, ordered, jnp.zeros_like(ordered))  8.33 us
  transfers between devices with their start and end apart: 2, of which 2 were waited for; matrix products, arithmetic and copies ran while one was open for 0% of the time, Pallas kernels for 0%

commit v1 on v0

--- a/solution.py
+++ b/solution.py
@@ -45,7 +45,9 @@
     moved = lax.all_to_all(ordered, "col", split_axis=3, concat_axis=1, tiled=True)
     amp_local = moved.reshape(irrep_local * VIR_CAP * OCC_CAP, moved.shape[3])
     amp_panel = lax.all_gather(amp_local, "row", axis=0, tiled=True)
-    ints_panel = lax.all_gather(cycle_ints, "col", axis=1, tiled=True)
+    ints_panel = jnp.concatenate(
+        lax.all_to_all(jnp.stack([cycle_ints] * lax.axis_size("col")), "col", 0, 0), axis=1
+    )
     cycle = jnp.dot(ints_panel, amp_panel, preferred_element_type=jnp.float32)
     rows_here = cycle.shape[0]
     cols_here = cycle.shape[1]

time: 409 us -> 455 us (1.11)
  waiting for transfers between devices: 289 us -> 338 us
  blocking collectives: 25.2 us -> 0 us
  starting transfers between devices: 0.04 us -> 14.3 us
  local copies, waits for them, and re-layouts: 61.7 us -> 69 us
    all_gather x1, waiting for transfers between devices: 166 us -> 322 us  [per_device(): amp_panel = lax.all_gather(amp_local, 'row', axis=0, tiled=True)]
    all_gather x1 -> x0, waiting for transfers between devices: 123 us -> none  [per_device(): ints_panel = lax.all_gather(cycle_ints, 'col', axis=1, tiled=True)]
    all_to_all x1 -> x0, blocking collectives: 25.2 us -> none  [per_device(): lax.all_to_all(ordered, 'col', split_axis=3, concat_axis=1, tiled=True)]
    all_to_all x0 -> x2, waiting for transfers between devices: none -> 16.7 us  [the longest x1 16.7 us: per_device(): lax.all_to_all(ordered, 'col', split_axis=3, concat_axis=1, tiled=True)]
    all_to_all x0 -> x2, starting transfers between devices: none -> 14.2 us  [the longest x1 8.45 us: per_device(): lax.all_to_all(ordered, 'col', split_axis=3, concat_axis=1, tiled=True)]
    another operation x0 -> x1, local copies, waits for them, and re-layouts: none -> 5.92 us  [per_device(): jnp.stack([cycle_ints] * lax.axis_size('col'))]
    unnamed x6 -> x9, local copies, waits for them, and re-layouts: 18 us -> 19.3 us
  transfers between devices with their start and end apart: 2 -> 3, of which waited for: 2 -> 2; matrix products, arithmetic and copies ran while one was open for 0% -> 4% of each run, Pallas kernels for 0% -> 0%
where the time goes in v1:
time: 455 us; the launch traced here: 454 us
  waiting for transfers between devices  338 us (74%)
  local copies, waits for them, and re-layouts  69 us (15%)
  matrix products  15.8 us (3%)
  starting transfers between devices  14.3 us (3%)
  between operations  14.2 us (3%)
    all_gather x1, waiting for transfers between devices, per_device(): amp_panel = lax.all_gather(amp_local, 'row', axis=0, tiled=True)  322 us
    unnamed x9, local copies, waits for them, and re-layouts  19.3 us
    all_to_all x1, waiting for transfers between devices, per_device(): lax.all_to_all(ordered, 'col', split_axis=3, concat_axis=1, tiled=True)  16.7 us
    dot_general x1, matrix products, per_device(): cycle = jnp.dot(ints_panel, amp_panel, preferred_element_type=jnp.float32)  15.6 us
    reshape x1, local copies, waits for them, and re-layouts, per_device(): jnp.transpose(t2_pairs, (0, 4, 2, 1, 5, 3))  15.1 us
    all_to_all x2, local copies, waits for them, and re-layouts, per_device(): lax.all_to_all(ordered, 'col', split_axis=3, concat_axis=1, tiled=True)  10.1 us
  transfers between devices with their start and end apart: 3, of which 2 were waited for; matrix products, arithmetic and copies ran while one was open for 4% of the time, Pallas kernels for 0%

profile of v1, /device:TPU:1, one launch (start us, length us, event | category | flops | bytes accessed | tf_op | source)
XLA Modules:
  0.0 453.9 jit_solution(9335281621856569683)
XLA Ops:
  6.5 0.0 copy-start
  7.2 0.8 select_reduce_fusion
  8.1 0.1 iota_compare_fusion.2
  8.1 0.7 iota_compare_fusion.3
  8.9 0.1 broadcast_and_fusion
  9.0 0.1 and.62
  9.2 7.9 %copy.23 = bf16[1,4,16,8,64,16]{5,4,3,2,1,0:T(8,128)(2,1)} copy(bf16[1,4,16,8,64,16]{4,1,5,2,3,0:T(4,128)(2,1)} %bitcast.26) | data formatting | bytes 2097152 | tf_op jit(solution)/shard_map/transpose | solution.py:40
  17.0 15.1 %reshape.114 = bf16[1,4,16,8192]{3,2,1,0:T(8,128)(2,1)S(1)} reshape(bf16[1,4,16,8,64,16]{5,4,3,2,1,0:T(8,128)(2,1)} %copy.23) | data formatting | bytes 2097152 | tf_op jit(solution)/shard_map/reshape | solution.py:40
  32.2 0.4 and_select_fusion
  32.6 0.0 copy-start.1
  32.6 8.3 %copy.24 = bf16[1,4,16,8192]{2,1,0,3:T(4,128)(2,1)} copy(bf16[1,4,16,8192]{3,2,1,0:T(8,128)(2,1)S(1)} %and_select_fusion) | data formatting | bytes 2097152 | tf_op jit(solution)/shard_map/jit(_where)/select_n | solution.py:44
  40.9 11.2 %reshape.118 = bf16[16,2,16384]{2,1,0:T(2,128)(2,1)} reshape(bf16[8192,1,4,16]{3,2,1,0:T(4,128)(2,1)} %bitcast.22) | data formatting | bytes 2097152
  52.2 8.4 %all-to-all-start = ((bf16[16,2,16384]{2,1,0:T(2,128)(2,1)}), bf16[16,2,16384]{2,1,0:T(2,128)(2,1)S(1)}, u32[]{:S(2)}, u32[]{:S(2)}) async-start(bf16[16,2,16384]{2,1,0:T(2,128)(2,1)} %reshape.118), calls=%async_computation | async-start | bytes 2097152 | tf_op jit(solution)/shard_map/all_to_all | solution.py:45
  60.6 0.0 copy-done.1
  60.6 0.5 copy.27
  61.2 16.7 %all-to-all-done = bf16[16,2,16384]{2,1,0:T(2,128)(2,1)S(1)} async-done(((bf16[16,2,16384]{2,1,0:T(2,128)(2,1)}), bf16[16,2,16384]{2,1,0:T(2,128)(2,1)S(1)}, u32[]{:S(2)}, u32[]{:S(2)}) %all-to-all-start) | async-done | bytes 1048608 | tf_op jit(solution)/shard_map/all_to_all | solution.py:45
  77.8 5.9 %stack.2 = bf16[16,1024,512]{1,2,0:T(8,128)(2,1)} broadcast(bf16[1024,512]{0,1:T(8,128)(2,1)S(1)} %copy.27), dimensions={1,2} | broadcast | bytes 17825792 | tf_op jit(solution)/shard_map/stack | solution.py:49
  83.7 5.8 %all-to-all-start.1 = ((bf16[16,1024,512]{1,2,0:T(8,128)(2,1)}), bf16[16,1024,512]{1,2,0:T(8,128)(2,1)}, u32[]{:S(2)}, u32[]{:S(2)}) async-start(bf16[16,1024,512]{1,2,0:T(8,128)(2,1)} %stack.2), calls=%async_computation.1 | async-start | bytes 33554432 | tf_op jit(solution)/shard_map/all_to_all | solution.py:49
  89.5 0.0 all-gather.2.cloned.1.call-start
  89.5 7.5 %reshape.119 = bf16[8192,1,4,16]{3,2,1,0:T(4,128)(2,1)} reshape(bf16[16,2,16384]{2,1,0:T(2,128)(2,1)S(1)} %all-to-all-done) | data formatting | bytes 2097152
  97.1 0.0 copy-start.2
  97.1 8.6 %copy.29 = bf16[1,4,16,16,512]{4,3,2,1,0:T(8,128)(2,1)S(1)} copy(bf16[1,4,16,16,512]{2,1,4,3,0:T(4,128)(2,1)} %bitcast.23) | data formatting | bytes 2097152 | tf_op jit(solution)/shard_map/all_to_all | solution.py:45
  105.7 1.5 copy.26
  107.2 0.0 all-gather.2.cloned.1.call-update
  107.3 0.1 dynamic_slice.16
  107.4 0.0 copy-done
  107.4 0.2 fusion.1
  107.5 0.0 copy-done.2
  107.5 0.1 broadcast_subtract_fusion
  107.7 0.1 sub.20
  107.8 0.1 dynamic_slice.19
  107.9 321.7 %all-gather.2.cloned.1.call-done = bf16[8192,512]{1,0:T(8,128)(2,1)} async-done(((bf16[1024,512]{1,0:T(8,128)(2,1)}), bf16[8192,512]{1,0:T(8,128)(2,1)}) %all-gather.2.cloned.1.call-update) | async-done | bytes 8388624 | tf_op jit(solution)/shard_map/all_gather | solution.py:47
  429.6 0.0 all-to-all-done.1
  429.6 15.6 %fusion = f32[1024,512]{0,1:T(8,128)S(1)} fusion(bf16[8192,512]{1,0:T(8,128)(2,1)} %all-gather.2.cloned.1.call-done, bf16[1024,8192]{0,1:T(8,128)(2,1)} %bitcast.7, f32[512]{0:T(512)S(1)} %dynamic_slice.19, f32[1024]{0:T(1024)S(1)} %dynamic_slice.18, pred[1024]{0:T(1024)(128)(4,1)S(1)} %dynamic_slice.15, pred[512]{0:T(512)(128)(4,1)S(1)} %dynamic_slice.16), kind=kOutput, calls=%fused_computation.1 | convolution fusion | flops 8592031744 | bytes 27270656 | tf_op jit(solution)/shard_map/dot_general | solution.py:51
  445.2 1.8 copy.28
  (4 shorter events, 0.0 us)
Async XLA Ops:
  6.5 100.8 %copy-start = (f32[8,64]{1,0:T(8,128)S(1)}, f32[8,64]{1,0:T(8,128)}, u32[]{:S(2)}) copy-start(f32[8,64]{1,0:T(8,128)} %param.10) | copy-start | bytes 6148
  32.6 28.0 %copy-start.1 = (bf16[1024,512]{1,0:T(8,128)(2,1)S(1)}, bf16[1024,512]{1,0:T(8,128)(2,1)}, u32[]{:S(2)}) copy-start(bf16[1024,512]{1,0:T(8,128)(2,1)} %param.8) | copy-start | bytes 3145732
  52.2 25.7 %all-to-all-start = ((bf16[16,2,16384]{2,1,0:T(2,128)(2,1)}), bf16[16,2,16384]{2,1,0:T(2,128)(2,1)S(1)}, u32[]{:S(2)}, u32[]{:S(2)}) async-start(bf16[16,2,16384]{2,1,0:T(2,128)(2,1)} %reshape.118), calls=%async_computation | async-start | bytes 2097152 | tf_op jit(solution)/shard_map/all_to_all | solution.py:45
  83.7 345.8 %all-to-all-start.1 = ((bf16[16,1024,512]{1,2,0:T(8,128)(2,1)}), bf16[16,1024,512]{1,2,0:T(8,128)(2,1)}, u32[]{:S(2)}, u32[]{:S(2)}) async-start(bf16[16,1024,512]{1,2,0:T(8,128)(2,1)} %stack.2), calls=%async_computation.1 | async-start | bytes 33554432 | tf_op jit(solution)/shard_map/all_to_all | solution.py:49
  89.5 340.1 %all-gather.2.cloned.1.call-start = ((), (), s32[]{:S(2)}) async-start(), calls=%async_computation.2 | async-start | bytes 9437184 | tf_op jit(solution)/shard_map/all_gather | solution.py:47
  97.1 10.5 %copy-start.2 = (f32[8,16]{1,0:T(8,128)S(1)}, f32[8,16]{1,0:T(8,128)}, u32[]{:S(2)}) copy-start(f32[8,16]{1,0:T(8,128)} %param.9) | copy-start | bytes 1540
Sparse Core Ops, SparseCore 0:
  107.4 322.1 all-gather.1

commit v2 on v0

--- a/solution.py
+++ b/solution.py
@@ -42,7 +42,10 @@
     )
     keep = source_live[:, :, :, None] & full_live[None, None, None, :]
     ordered = jnp.where(keep, ordered, jnp.zeros_like(ordered))
-    moved = lax.all_to_all(ordered, "col", split_axis=3, concat_axis=1, tiled=True)
+    moved = jnp.concatenate(
+        lax.all_to_all(jnp.stack(jnp.split(ordered, lax.axis_size("col"), axis=3)), "col", 0, 0),
+        axis=1,
+    )
     amp_local = moved.reshape(irrep_local * VIR_CAP * OCC_CAP, moved.shape[3])
     amp_panel = lax.all_gather(amp_local, "row", axis=0, tiled=True)
     ints_panel = lax.all_gather(cycle_ints, "col", axis=1, tiled=True)

time: 409 us -> 373 us (0.912)
  local copies, waits for them, and re-layouts: 61.7 us -> 25.4 us
    unnamed x6 -> x19, local copies, waits for them, and re-layouts: 18 us -> 0.11 us
    all_to_all x2 -> x0, local copies, waits for them, and re-layouts: 10.1 us -> none  [per_device(): lax.all_to_all(ordered, 'col', split_axis=3, concat_axis=1, tiled=True)]
    select_n x1 -> x0, local copies, waits for them, and re-layouts: 8.33 us -> none  [per_device(): ordered = jnp.where(keep, ordered, jnp.zeros_like(ordered))]
where the time goes in v2:
time: 373 us; the launch traced here: 372 us
  waiting for transfers between devices  289 us (77%)
  local copies, waits for them, and re-layouts  25.4 us (7%)
  blocking collectives  25.3 us (7%)
  matrix products  15.9 us (4%)
  between operations  14.3 us (4%)
    all_gather x1, waiting for transfers between devices, per_device(): amp_panel = lax.all_gather(amp_local, 'row', axis=0, tiled=True)  166 us
    all_gather x1, waiting for transfers between devices, per_device(): ints_panel = lax.all_gather(cycle_ints, 'col', axis=1, tiled=True)  123 us
    all_to_all x1, blocking collectives, per_device(): lax.all_to_all(jnp.stack(jnp.split(ordered, lax.axis_size('col'), axis=3)...  25.3 us
    dot_general x1, matrix products, per_device(): cycle = jnp.dot(ints_panel, amp_panel, preferred_element_type=jnp.float32)  15.7 us
    reshape x1, local copies, waits for them, and re-layouts, per_device(): jnp.transpose(t2_pairs, (0, 4, 2, 1, 5, 3))  15.1 us
    transpose x1, local copies, waits for them, and re-layouts, per_device(): jnp.transpose(t2_pairs, (0, 4, 2, 1, 5, 3))  7.88 us
  transfers between devices with their start and end apart: 2, of which 2 were waited for; matrix products, arithmetic and copies ran while one was open for 0% of the time, Pallas kernels for 0%

profile of v2, /device:TPU:1, one launch (start us, length us, event | category | flops | bytes accessed | tf_op | source)
XLA Modules:
  0.0 372.2 jit_solution(2108434927644377425)
XLA Ops:
  6.5 0.0 copy-start
  6.5 0.0 all-gather.3.cloned.1.call-start
  7.2 0.8 select_reduce_fusion
  8.1 0.1 iota_compare_fusion.2
  8.1 0.7 iota_compare_fusion.3
  8.9 0.1 broadcast_and_fusion
  9.0 0.1 and.62
  9.2 7.9 %copy.11 = bf16[1,4,16,8,64,16]{5,4,3,2,1,0:T(8,128)(2,1)} copy(bf16[1,4,16,8,64,16]{4,1,5,2,3,0:T(4,128)(2,1)} %bitcast.80) | data formatting | bytes 2097152 | tf_op jit(solution)/shard_map/transpose | solution.py:40
  17.0 15.1 %reshape.102 = bf16[1,4,16,8192]{3,2,1,0:T(8,128)(2,1)S(1)} reshape(bf16[1,4,16,8,64,16]{5,4,3,2,1,0:T(8,128)(2,1)} %copy.11) | data formatting | bytes 2097152 | tf_op jit(solution)/shard_map/reshape | solution.py:40
  32.2 0.4 and_select_fusion
  32.8 0.0 copy-start.1
  32.8 25.3 %all_to_all.5 = bf16[16,1,4,16,512]{4,3,2,1,0:T(8,128)(2,1)} all-to-all(bf16[16,1,4,16,512]{4,3,2,1,0:T(8,128)(2,1)S(1)} %fusion.1), channel_id=1, replica_groups=mesh['row'=8,'col'=16] {'col'}, dimensions={0} | all-to-all | bytes 2097152 | tf_op jit(solution)/shard_map/all_to_all | solution.py:46
  58.1 0.0 all-gather.3.cloned.1.call-update
  58.1 0.0 all-gather.5.cloned.1.call-start
  58.2 0.7 all-gather.5.cloned.1.call-update
  58.9 0.1 dynamic_slice.16
  59.0 0.0 copy-done
  59.0 0.2 fusion.17
  59.1 0.0 copy-done.1
  59.1 0.1 broadcast_subtract_fusion
  59.3 0.1 sub.20
  59.4 0.1 dynamic_slice.19
  59.5 165.7 %all-gather.3.cloned.1.call-done = bf16[8192,512]{1,0:T(8,128)(2,1)} async-done(((bf16[1024,512]{1,0:T(8,128)(2,1)}), bf16[8192,512]{1,0:T(8,128)(2,1)}) %all-gather.3.cloned.1.call-update) | async-done | bytes 8388624 | tf_op jit(solution)/shard_map/all_gather | solution.py:50
  225.2 122.6 %all-gather.5.cloned.1.call-done = bf16[1024,8192]{1,0:T(8,128)(2,1)} async-done(((bf16[1024,512]{1,0:T(8,128)(2,1)}), bf16[1024,8192]{1,0:T(8,128)(2,1)}) %all-gather.5.cloned.1.call-update) | async-done | bytes 16777232 | tf_op jit(solution)/shard_map/all_gather | solution.py:51
  347.9 15.7 %fusion = f32[1024,512]{0,1:T(8,128)S(1)} fusion(bf16[8192,512]{1,0:T(8,128)(2,1)} %all-gather.3.cloned.1.call-done, bf16[1024,8192]{1,0:T(8,128)(2,1)} %all-gather.5.cloned.1.call-done, f32[512]{0:T(512)S(1)} %dynamic_slice.19, f32[1024]{0:T(1024)S(1)} %dynamic_slice.18, pred[1024]{0:T(1024)(128)(4,1)S(1)} %dynamic_slice.15, ...), kind=kOutput, calls=%fused_computation.1 | convolution fusion | flops 8592031744 | bytes 27270656 | tf_op jit(solution)/shard_map/dot_general | solution.py:52
  363.6 1.8 copy.12
  (20 shorter events, 0.1 us)
Async XLA Ops:
  6.5 52.4 %copy-start = (f32[8,64]{1,0:T(8,128)S(1)}, f32[8,64]{1,0:T(8,128)}, u32[]{:S(2)}) copy-start(f32[8,64]{1,0:T(8,128)} %param.10) | copy-start | bytes 6148
  6.5 218.7 %all-gather.3.cloned.1.call-start = ((), (), s32[]{:S(2)}) async-start(), calls=%async_computation.1 | async-start | bytes 9437184 | tf_op jit(solution)/shard_map/all_gather | solution.py:50
  32.8 26.3 %copy-start.1 = (f32[8,16]{1,0:T(8,128)S(1)}, f32[8,16]{1,0:T(8,128)}, u32[]{:S(2)}) copy-start(f32[8,16]{1,0:T(8,128)} %param.9) | copy-start | bytes 1540
  58.1 289.7 %all-gather.5.cloned.1.call-start = ((), (), s32[]{:S(2)}) async-start(), calls=%async_computation.2 | async-start | bytes 17825792 | tf_op jit(solution)/shard_map/all_gather | solution.py:51
Sparse Core Ops, SparseCore 0:
  58.2 166.9 all-gather.2
  227.5 120.3 all-gather.4
